TPU v7x, 32 devices: a whole 2x2x4 slice. The times are simulated.
32 devices in a mesh: dp: 8 (over y, x, core), tensor: 4 (over z).
Axes of the slice: x: 2, y: 2, z: 4, core: 2. Of those that a mesh axis runs over, the one named last changes fastest.
Arguments:
- tokens: bfloat16 [16384, 768], P('dp'), may hold values from -6 to 6
- doc_lengths: int32 [16, 8], P('dp'), may hold values from 1 to 512, 1024 in all within a row
- wq: bfloat16 [768, 768], P('dp', 'tensor'), may hold values from -0.21875 to 0.21875
- bq: float32 [768], P('tensor'), may hold values from -3 to 3
- wk: bfloat16 [768, 768], P('dp', 'tensor'), may hold values from -0.21875 to 0.21875
- wv: bfloat16 [768, 768], P('dp', 'tensor'), may hold values from -0.21875 to 0.21875
- bv: float32 [768], P('tensor'), may hold values from -3 to 3
- wo: bfloat16 [768, 768], P('tensor', 'dp'), may hold values from -0.875 to 0.875
- bo: float32 [768], replicated, may hold values from -3 to 3
- gain1: float32 [768], replicated, may hold values from 0.25 to 1.75
- shift1: float32 [768], replicated, may hold values from -3 to 3
- w1: bfloat16 [768, 3072], P('dp', 'tensor'), may hold values from -0.21875 to 0.21875
- b1: float32 [3072], P('tensor'), may hold values from -3 to 3
- w2: bfloat16 [3072, 768], P('tensor', 'dp'), may hold values from -0.109375 to 0.109375
- b2: float32 [768], replicated, may hold values from -3 to 3
- gain2: float32 [768], replicated, may hold values from 0.25 to 1.75
- shift2: float32 [768], replicated, may hold values from -3 to 3
- cotangent: bfloat16 [16384, 768], P('dp'), may hold values from -6 to 6
Outputs:
- out: bfloat16 [16384, 768], P('dp')
- grad_tokens: bfloat16 [16384, 768], P('dp')
- grad_wq: float32 [768, 768], P('dp', 'tensor')
- grad_bq: float32 [768], P('tensor')
- grad_wk: float32 [768, 768], P('dp', 'tensor')
- grad_wv: float32 [768, 768], P('dp', 'tensor')
- grad_bv: float32 [768], P('tensor')
- grad_wo: float32 [768, 768], P('tensor', 'dp')
- grad_bo: float32 [768], replicated
- grad_gain1: float32 [768], replicated
- grad_shift1: float32 [768], replicated
- grad_w1: float32 [768, 3072], P('dp', 'tensor')
- grad_b1: float32 [3072], P('tensor')
- grad_w2: float32 [3072, 768], P('tensor', 'dp')
- grad_b2: float32 [768], replicated
- grad_gain2: float32 [768], replicated
- grad_shift2: float32 [768], replicated
Inputs may be any that keep to these rules, and one draw needn't show every extreme that they name: `doc_lengths`: row s holds the lengths of the documents packed in order into sequence s; each row sums to 1024.
All inputs are finite; a program needn't handle non-finite values.
Results may differ from a plain program's by a relative error of at most 0.02.
Values may be sent and summed in bfloat16 or wider, within the bound.
A program may use at most 192 MiB of HBM per device.

v0:
```python
from functools import partial
import jax
import jax.numpy as jnp
from jax import lax
from jax.sharding import PartitionSpec as P

HD = 64
eps_norm = 1e-12
masked_score = -1e30


def doc_ids(lengths, count):
    ends = jnp.cumsum(lengths)
    places = jnp.arange(count, dtype=jnp.int32)
    return jnp.sum((places[:, None] >= ends[None, :]).astype(jnp.int32), axis=1)


def collect(wq, wk, wv, wo, w1, w2):
    return (
        lax.all_gather(wq, "dp", axis=0, tiled=True),
        lax.all_gather(wk, "dp", axis=0, tiled=True),
        lax.all_gather(wv, "dp", axis=0, tiled=True),
        lax.all_gather(wo, "dp", axis=1, tiled=True),
        lax.all_gather(w1, "dp", axis=0, tiled=True),
        lax.all_gather(w2, "dp", axis=1, tiled=True),
    )


def reduce_large(grads):
    return (
        lax.psum_scatter(grads[0], "dp", scatter_dimension=0, tiled=True),
        lax.psum_scatter(grads[1], "dp", scatter_dimension=0, tiled=True),
        lax.psum_scatter(grads[2], "dp", scatter_dimension=0, tiled=True),
        lax.psum_scatter(grads[3], "dp", scatter_dimension=1, tiled=True),
        lax.psum_scatter(grads[4], "dp", scatter_dimension=0, tiled=True),
        lax.psum_scatter(grads[5], "dp", scatter_dimension=1, tiled=True),
    )


def reduce_small(grads):
    return lax.psum(
        (grads[0], grads[1], grads[2], grads[3], grads[4], grads[5], grads[6], grads[7], grads[8]),
        "dp",
    )


def contract_rows(left, right):
    return lax.dot_general(
        left, right, (((0,), (0,)), ((), ())), preferred_element_type=jnp.float32
    )


def contract_cols(left, right):
    return lax.dot_general(
        left, right, (((1,), (1,)), ((), ())), preferred_element_type=jnp.float32
    )


def contract_mixed(left, right):
    return lax.dot_general(
        left, right, (((0,), (1,)), ((), ())), preferred_element_type=jnp.float32
    )


def norm_forward(total, gain, shift):
    centre = total - jnp.mean(total, axis=-1, keepdims=True)
    scaled = lax.rsqrt(jnp.mean(centre * centre, axis=-1, keepdims=True) + eps_norm)
    normed = centre * scaled
    return (normed * gain + shift, normed, scaled)


def norm_backward(grad_result, normed, scaled, gain):
    grad_normed = grad_result * gain
    mean_grad = jnp.mean(grad_normed, axis=-1, keepdims=True)
    mean_cross = jnp.mean(grad_normed * normed, axis=-1, keepdims=True)
    grad_total = scaled * (grad_normed - mean_grad - normed * mean_cross)
    return (grad_total, jnp.sum(grad_result * normed, axis=0), jnp.sum(grad_result, axis=0))


def block_scores(query_block, key_heads, seg_block, seg, scale):
    raw = (
        jnp.einsum("hdq,hdk->hqk", query_block, key_heads, preferred_element_type=jnp.float32)
        * scale
    )
    same_doc = seg_block[:, None] == seg[None, :]
    return jnp.where(same_doc[None], raw, masked_score)


def body(
    tokens,
    doc_lengths,
    wq,
    bq,
    wk,
    wv,
    bv,
    wo,
    bo,
    gain1,
    shift1,
    w1,
    b1,
    w2,
    b2,
    gain2,
    shift2,
    cotangent,
):
    micro = doc_lengths.shape[0]
    seq_len = tokens.shape[0] // micro
    block = min(512, seq_len)
    scale = HD ** (-0.5)
    results = []
    grad_inputs = []
    large_total = None
    small_total = None
    for index in range(micro):
        full = collect(wq, wk, wv, wo, w1, w2)
        full_q, full_k, full_v, full_o, full_first, full_second = full
        width = full_q.shape[1]
        heads_here = width // HD
        rows_in = tokens[index * seq_len : (index + 1) * seq_len]
        inputs = rows_in.astype(jnp.float32)
        seg = doc_ids(doc_lengths[index], seq_len)
        queries = (
            lax.dot_general(
                full_q, rows_in, (((0,), (1,)), ((), ())), preferred_element_type=jnp.float32
            )
            + bq[:, None]
        ).astype(jnp.bfloat16)
        keys_low = lax.dot_general(
            full_k, rows_in, (((0,), (1,)), ((), ())), preferred_element_type=jnp.float32
        ).astype(jnp.bfloat16)
        values_low = (
            lax.dot_general(
                full_v, rows_in, (((0,), (1,)), ((), ())), preferred_element_type=jnp.float32
            )
            + bv[:, None]
        ).astype(jnp.bfloat16)
        query_heads = queries.reshape(heads_here, HD, seq_len)
        key_heads = keys_low.reshape(heads_here, HD, seq_len)
        value_heads = values_low.reshape(heads_here, HD, seq_len)
        pieces = []
        log_totals = []
        for offset in range(0, seq_len, block):
            scores = block_scores(
                query_heads[:, :, offset : offset + block],
                key_heads,
                seg[offset : offset + block],
                seg,
                scale,
            )
            highest = jnp.max(scores, axis=-1, keepdims=True)
            log_total = highest + jnp.log(
                jnp.sum(jnp.exp(scores - highest), axis=-1, keepdims=True)
            )
            probs_low = jnp.exp(scores - log_total).astype(jnp.bfloat16)
            pieces.append(
                jnp.einsum(
                    "hqk,hdk->hdq", probs_low, value_heads, preferred_element_type=jnp.float32
                )
            )
            log_totals.append(log_total)
        mixed_cols = jnp.concatenate(pieces, axis=2).reshape(width, seq_len).astype(jnp.bfloat16)
        attended = lax.psum(
            contract_rows(mixed_cols, full_o).astype(jnp.bfloat16), "tensor"
        ).astype(jnp.float32)
        first, normed_one, scaled_one = norm_forward(inputs + attended + bo, gain1, shift1)
        first_low = first.astype(jnp.bfloat16)
        inner = jnp.dot(first_low, full_first, preferred_element_type=jnp.float32) + b1
        hidden = jax.nn.gelu(inner, approximate=False).astype(jnp.bfloat16)
        second = lax.psum(
            jnp.dot(hidden, full_second, preferred_element_type=jnp.float32).astype(jnp.bfloat16),
            "tensor",
        ).astype(jnp.float32)
        result, normed_two, scaled_two = norm_forward(first + second + b2, gain2, shift2)
        results.append(result.astype(jnp.bfloat16))
        grad_result = cotangent[index * seq_len : (index + 1) * seq_len].astype(jnp.float32)
        grad_two, grad_gain2, grad_shift2 = norm_backward(
            grad_result, normed_two, scaled_two, gain2
        )
        grad_b2 = jnp.sum(grad_two, axis=0)
        full = collect(wq, wk, wv, wo, w1, w2)
        full_q, full_k, full_v, full_o, full_first, full_second = full
        two_low = grad_two.astype(jnp.bfloat16)
        grad_w2 = contract_rows(hidden, two_low)
        grad_hidden = contract_cols(two_low, full_second)
        grad_inner = jax.vjp(partial(jax.nn.gelu, approximate=False), inner)[1](grad_hidden)[
            0
        ].astype(jnp.bfloat16)
        grad_b1 = jnp.sum(grad_inner.astype(jnp.float32), axis=0)
        grad_w1 = contract_rows(first_low, grad_inner)
        grad_first = grad_two + lax.psum(
            contract_cols(grad_inner, full_first).astype(jnp.bfloat16), "tensor"
        ).astype(jnp.float32)
        grad_one, grad_gain1, grad_shift1 = norm_backward(grad_first, normed_one, scaled_one, gain1)
        grad_bo = jnp.sum(grad_one, axis=0)
        one_low = grad_one.astype(jnp.bfloat16)
        grad_wo = jnp.dot(mixed_cols, one_low, preferred_element_type=jnp.float32)
        grad_mixed = (
            contract_cols(full_o, one_low).astype(jnp.bfloat16).reshape(heads_here, HD, seq_len)
        )
        grad_key_heads = jnp.zeros((heads_here, HD, seq_len), jnp.float32)
        grad_value_heads = jnp.zeros((heads_here, HD, seq_len), jnp.float32)
        grad_query_pieces = []
        for number, offset in enumerate(range(0, seq_len, block)):
            query_block = query_heads[:, :, offset : offset + block]
            grad_block = grad_mixed[:, :, offset : offset + block]
            scores = block_scores(query_block, key_heads, seg[offset : offset + block], seg, scale)
            probs = jnp.exp(scores - log_totals[number])
            grad_probs = jnp.einsum(
                "hdq,hdk->hqk", grad_block, value_heads, preferred_element_type=jnp.float32
            )
            centre = jnp.sum(probs * grad_probs, axis=-1, keepdims=True)
            grad_scores = (probs * (grad_probs - centre)).astype(jnp.bfloat16)
            grad_query_pieces.append(
                jnp.einsum(
                    "hqk,hdk->hdq", grad_scores, key_heads, preferred_element_type=jnp.float32
                )
                * scale
            )
            grad_key_heads = (
                grad_key_heads
                + jnp.einsum(
                    "hqk,hdq->hdk", grad_scores, query_block, preferred_element_type=jnp.float32
                )
                * scale
            )
            grad_value_heads = grad_value_heads + jnp.einsum(
                "hqk,hdq->hdk",
                probs.astype(jnp.bfloat16),
                grad_block,
                preferred_element_type=jnp.float32,
            )
        grad_queries = (
            jnp.concatenate(grad_query_pieces, axis=2).reshape(width, seq_len).astype(jnp.bfloat16)
        )
        grad_keys = grad_key_heads.reshape(width, seq_len).astype(jnp.bfloat16)
        grad_values = grad_value_heads.reshape(width, seq_len).astype(jnp.bfloat16)
        grad_bq = jnp.sum(grad_queries.astype(jnp.float32), axis=1)
        grad_bv = jnp.sum(grad_values.astype(jnp.float32), axis=1)
        grad_wq = contract_cols(rows_in.T, grad_queries)
        grad_wk = contract_cols(rows_in.T, grad_keys)
        grad_wv = contract_cols(rows_in.T, grad_values)
        back_terms = (
            contract_mixed(grad_queries, full_q)
            + contract_mixed(grad_keys, full_k)
            + contract_mixed(grad_values, full_v)
        )
        grad_rows = grad_one + lax.psum(back_terms.astype(jnp.bfloat16), "tensor").astype(
            jnp.float32
        )
        grad_inputs.append(grad_rows.astype(jnp.bfloat16))
        large_local = (grad_wq, grad_wk, grad_wv, grad_wo, grad_w1, grad_w2)
        small_local = (
            grad_bq,
            grad_bv,
            grad_b1,
            grad_bo,
            grad_b2,
            grad_gain1,
            grad_shift1,
            grad_gain2,
            grad_shift2,
        )
        large_local = reduce_large(large_local)
        small_local = reduce_small(small_local)
        if large_total is None:
            large_total = large_local
            small_total = small_local
        else:
            large_total = jax.tree.map(jnp.add, large_total, large_local)
            small_total = jax.tree.map(jnp.add, small_total, small_local)
    grad_wq, grad_wk, grad_wv, grad_wo, grad_w1, grad_w2 = large_total
    (
        grad_bq,
        grad_bv,
        grad_b1,
        grad_bo,
        grad_b2,
        grad_gain1,
        grad_shift1,
        grad_gain2,
        grad_shift2,
    ) = small_total
    return (
        jnp.concatenate(results, axis=0),
        jnp.concatenate(grad_inputs, axis=0),
        grad_wq,
        grad_bq,
        grad_wk,
        grad_wv,
        grad_bv,
        grad_wo,
        grad_bo,
        grad_gain1,
        grad_shift1,
        grad_w1,
        grad_b1,
        grad_w2,
        grad_b2,
        grad_gain2,
        grad_shift2,
    )


def solution(mesh):
    placed = (
        P("dp", None),
        P("dp", None),
        P("dp", "tensor"),
        P("tensor"),
        P("dp", "tensor"),
        P("dp", "tensor"),
        P("tensor"),
        P("tensor", "dp"),
        P(),
        P(),
        P(),
        P("dp", "tensor"),
        P("tensor"),
        P("tensor", "dp"),
        P(),
        P(),
        P(),
        P("dp", None),
    )
    return jax.shard_map(
        body,
        mesh=mesh,
        in_specs=placed,
        out_specs=(
            P("dp", None),
            P("dp", None),
            P("dp", "tensor"),
            P("tensor"),
            P("dp", "tensor"),
            P("dp", "tensor"),
            P("tensor"),
            P("tensor", "dp"),
            P(),
            P(),
            P(),
            P("dp", "tensor"),
            P("tensor"),
            P("tensor", "dp"),
            P(),
            P(),
            P(),
        ),
        check_vma=False,
    )
```

profile of v0, /device:TPU:0, one launch (start us, length us, event | category | flops | bytes accessed | tf_op | source)
XLA Modules:
  0.0 842.3 jit_solution(16882995216697023067)
XLA Ops:
  8.1 11.6 %all_gather.12 = bf16[768,192]{1,0:T(8,128)(2,1)S(1)} all-gather(bf16[96,192]{1,0:T(8,128)(2,1)} %param.23), channel_id=1, replica_groups=mesh['dp'=8,'tensor'=4] {'dp'}, dimensions={0}, use_global_device_ids=true | all-gather | bytes 331776 | tf_op jit(solution)/shard_map/all_gather | solution.py:22
  19.7 3.0 fusion.49
  24.1 9.4 %all_gather.14 = bf16[768,192]{1,0:T(8,128)(2,1)S(1)} all-gather(bf16[96,192]{1,0:T(8,128)(2,1)S(1)} %copy-done.92), channel_id=1, replica_groups=mesh['dp'=8,'tensor'=4] {'dp'}, dimensions={0}, use_global_device_ids=true | all-gather | bytes 331776 | tf_op jit(solution)/shard_map/all_gather | solution.py:21
  36.5 9.0 %all_gather.13 = bf16[768,192]{1,0:T(8,128)(2,1)S(1)} all-gather(bf16[96,192]{1,0:T(8,128)(2,1)S(1)} %copy-done.93), channel_id=1, replica_groups=mesh['dp'=8,'tensor'=4] {'dp'}, dimensions={0}, use_global_device_ids=true | all-gather | bytes 331776 | tf_op jit(solution)/shard_map/all_gather | solution.py:20
  50.2 9.3 %all_gather.15 = bf16[192,768]{0,1:T(8,128)(2,1)S(1)} all-gather(bf16[192,96]{0,1:T(8,128)(2,1)} %copy.42), channel_id=1, replica_groups=mesh['dp'=8,'tensor'=4] {'dp'}, dimensions={1}, use_global_device_ids=true | all-gather | bytes 331776 | tf_op jit(solution)/shard_map/all_gather | solution.py:23
  60.9 2.8 fusion.2
  90.3 120.7 %all-reduce.16.cloned.1.call-done = (bf16[1024,768]{1,0:T(8,128)(2,1)}, bf16[1024,768]{1,0:T(8,128)(2,1)}) async-done(((bf16[1024,768]{1,0:T(8,128)(2,1)}, bf16[1024,768]{1,0:T(8,128)(2,1)}), (bf16[1024,768]{1,0:T(8,128)(2,1)}, bf16[1024,768]{1,0:T(8,128)(2,1)})) %all-reduce.16.cloned.1.call-update) | async-done | bytes 3145744 | tf_op jit(solution)/shard_map/psum | solution.py:165
  216.2 3.8 fusion.68
  221.7 17.1 %multiply_convert_fusion.5 = (bf16[1024,768]{1,0:T(8,128)(2,1)}, f32[1024,768]{1,0:T(8,128)}, bf16[1024,768]{1,0:T(8,128)(2,1)}, f32[1024,768]{1,0:T(8,128)}, f32[1024,768]{1,0:T(8,128)}) fusion(f32[768]{0:T(1024)S(1)} %copy-done.119, f32[1024,768]{1,0:T(8,128)S(1)} %fusion.68, bf16[768,768]{1,0:T(8,128)(2,1)S(1)} %copy-done.115, f32[768]{0:T(1024)S(1)} %copy-done.110, ...), kind=kOutput, calls=%fused_computation.92 | convolution fusion | flops 1318846464 | bytes 20078592 | tf_op jit(solution)/shard_map/dot_general | solution.py:170
  238.9 4.5 convolution_convert_fusion.4
  243.3 2.6 convolution_convert_fusion.2
  246.0 120.6 %all-reduce.14.cloned.1.call-done = (bf16[1024,768]{1,0:T(8,128)(2,1)}, bf16[1024,768]{1,0:T(8,128)(2,1)}) async-done(((bf16[1024,768]{1,0:T(8,128)(2,1)}, bf16[1024,768]{1,0:T(8,128)(2,1)}), (bf16[1024,768]{1,0:T(8,128)(2,1)}, bf16[1024,768]{1,0:T(8,128)(2,1)})) %all-reduce.14.cloned.1.call-update) | async-done | bytes 3145744 | tf_op jit(solution)/shard_map/psum | solution.py:172
  366.5 5.4 fusion.131
  373.8 3.5 convert_reduce_fusion
  377.4 4.3 fusion.18
  381.8 2.9 convert_reduce_fusion.2
  384.7 2.6 convolution_convert_fusion
  388.6 2.9 convert_reduce_fusion.3
  392.6 2.6 convolution_convert_fusion.1
  395.3 120.6 %all-reduce.12.cloned.1.call-done = (bf16[1024,768]{1,0:T(8,128)(2,1)}, bf16[1024,768]{1,0:T(8,128)(2,1)}) async-done(((bf16[1024,768]{1,0:T(8,128)(2,1)}, bf16[1024,768]{1,0:T(8,128)(2,1)}), (bf16[1024,768]{1,0:T(8,128)(2,1)}, bf16[1024,768]{1,0:T(8,128)(2,1)})) %all-reduce.12.cloned.1.call-update) | async-done | bytes 3145744 | tf_op jit(solution)/shard_map/psum | solution.py:193
  515.9 9.4 %multiply_reduce_fusion.5 = (f32[768]{0:T(1024)}, f32[1024]{0:T(1024)S(1)}, f32[1024]{0:T(1024)S(1)}, f32[768]{0:T(1024)}, f32[768]{0:T(1024)}, /*index=5*/f32[1...) fusion(f32[1024,768]{1,0:T(8,128)} %copy-done.18, bf16[1024,768]{1,0:T(8,128)(2,1)} %get-tuple-element.110, ...), kind=kLoop, calls=%fused_computation.57 | loop fusion | flops 24371456 | bytes 15782912 | tf_op jit(solution)/shard_map/reduce_sum | solution.py:77
  525.4 5.3 fusion.130
  534.6 2.7 fusion.77
  537.4 4.4 multiply_reduce_fusion
  541.8 4.3 multiply_reduce_fusion.1
  546.1 8.4 multiply_convert_fusion
  554.6 3.8 convolution_multiply_fusion.1
  560.1 5.7 fusion.84
  565.9 4.4 multiply_reduce_fusion.2
  570.3 4.4 multiply_reduce_fusion.3
  574.7 8.2 multiply_convert_fusion.2
  582.9 3.8 convolution_multiply_fusion.3
  592.4 5.8 convert_reduce_fusion.4
  598.2 5.6 convert_reduce_fusion.5
  616.7 4.0 fusion.61
  620.8 3.0 convolution_add_fusion
  623.9 4.0 fusion.70
  627.9 3.5 convolution_add_fusion.1
  634.3 2.3 copy.50
  642.0 2.2 copy.46
  644.4 3.8 pad_maximum_fusion
  652.3 2.2 copy.48
  656.6 26.5 %all-reduce = (f32[192]{0:T(256)}, f32[192]{0:T(256)}, f32[768]{0:T(1024)}, f32[768]{0:T(1024)}, f32[768]{0:T(1024)}, /*index=5*/f32[768]{0:T(1024)}, f32[768]{0:T(1024)}, f32[768]{0:T(1024)}, f32[768]{0:T(1024)}) all-reduce(f32[192]{0:T(256)} %reshape.371, f32[192]{0:T(256)} %reshape.372, ...), channel_id=1, replica_groups=mesh['dp'=8,'tensor'=4] {'dp'}, use_global_device_ids=true, to_apply=%region_43.44 | all-reduce | flops 5760 | bytes 46080 | tf_op jit(solution)/shard_map/psum | solution.py:41
  684.8 52.3 %all-reduce.10.cloned.1.call-done = (bf16[1024,768]{1,0:T(8,128)(2,1)}, bf16[1024,768]{1,0:T(8,128)(2,1)}) async-done(((bf16[1024,768]{1,0:T(8,128)(2,1)}, bf16[1024,768]{1,0:T(8,128)(2,1)}), (bf16[1024,768]{1,0:T(8,128)(2,1)}, bf16[1024,768]{1,0:T(8,128)(2,1)})) %all-reduce.10.cloned.1.call-update) | async-done | bytes 3145744 | tf_op jit(solution)/shard_map/psum | solution.py:250
  737.1 2.8 add_convert_fusion.3
  743.1 14.7 %reduce-scatter.23.cloned.1.call-done = f32[96,192]{1,0:T(8,128)} async-done(((f32[768,192]{1,0:T(8,128)}), f32[96,192]{1,0:T(8,128)}) %reduce-scatter.23.cloned.1.call-update) | async-done | bytes 73744
  757.8 38.6 %reduce-scatter.19.cloned.1.call-done = f32[96,192]{1,0:T(8,128)} async-done(((f32[768,192]{1,0:T(8,128)}), f32[96,192]{1,0:T(8,128)}) %reduce-scatter.19.cloned.1.call-update) | async-done | bytes 73744
  796.4 38.6 %reduce-scatter.21.cloned.1.call-done = f32[96,192]{1,0:T(8,128)} async-done(((f32[768,192]{1,0:T(8,128)}), f32[96,192]{1,0:T(8,128)}) %reduce-scatter.21.cloned.1.call-update) | async-done | bytes 73744
  (411 shorter events, 91.5 us)
Async XLA Ops:
  8.0 14.6 %copy-start = (bf16[2048,768]{1,0:T(8,128)(2,1)S(1)}, bf16[2048,768]{1,0:T(8,128)(2,1)}, u32[]{:S(2)}) copy-start(bf16[2048,768]{1,0:T(8,128)(2,1)} %param.18) | copy-start | bytes 9437188
  8.0 14.6 %copy-start.121 = (f32[192]{0:T(256)S(1)}, f32[192]{0:T(256)}, u32[]{:S(2)}) copy-start(f32[192]{0:T(256)} %param.24) | copy-start | bytes 2308
  8.0 16.1 %copy-start.92 = (bf16[96,192]{1,0:T(8,128)(2,1)S(1)}, bf16[96,192]{1,0:T(8,128)(2,1)}, u32[]{:S(2)}) copy-start(bf16[96,192]{1,0:T(8,128)(2,1)} %param.22) | copy-start | bytes 110596
  8.1 202.9 %all-reduce.16.cloned.1.call-start = ((), (), s32[]{:S(2)}) async-start(), calls=%async_computation.17 | async-start | bytes 6291456 | tf_op jit(solution)/shard_map/psum | solution.py:165
  19.7 13.9 %copy-start.40 = (bf16[768,192]{1,0:T(8,128)(2,1)}, bf16[768,192]{1,0:T(8,128)(2,1)S(1)}, u32[]{:S(2)}) copy-start(bf16[768,192]{1,0:T(8,128)(2,1)S(1)} %all_gather.12) | copy-start | bytes 884740
  24.1 12.3 %copy-start.93 = (bf16[96,192]{1,0:T(8,128)(2,1)S(1)}, bf16[96,192]{1,0:T(8,128)(2,1)}, u32[]{:S(2)}) copy-start(bf16[96,192]{1,0:T(8,128)(2,1)} %param.20) | copy-start | bytes 110596
  24.1 21.3 %copy-start.122 = (f32[192]{0:T(256)S(1)}, f32[192]{0:T(256)}, u32[]{:S(2)}) copy-start(f32[192]{0:T(256)} %param.21) | copy-start | bytes 2308
  33.6 13.3 %copy-start.52 = (bf16[768,192]{1,0:T(8,128)(2,1)}, bf16[768,192]{1,0:T(8,128)(2,1)S(1)}, u32[]{:S(2)}) copy-start(bf16[768,192]{1,0:T(8,128)(2,1)S(1)} %all_gather.14) | copy-start | bytes 884740
  36.4 11.9 %copy-start.114 = (s32[2,8]{1,0:T(2,128)S(1)}, s32[2,8]{1,0:T(2,128)}, u32[]{:S(2)}) copy-start(s32[2,8]{1,0:T(2,128)} %param.19) | copy-start | bytes 196
  36.5 13.0 %copy-start.94 = (bf16[192,96]{1,0:T(8,128)(2,1)S(1)}, bf16[192,96]{1,0:T(8,128)(2,1)}, u32[]{:S(2)}) copy-start(bf16[192,96]{1,0:T(8,128)(2,1)} %param.25) | copy-start | bytes 110596
  60.9 8.0 copy-start.29
  60.9 10.0 %copy-start.24 = (pred[512,1024]{1,0:T(8,128)(4,1)}, pred[512,1024]{1,0:T(8,128)(4,1)S(1)}, u32[]{:S(2)}) copy-start(pred[512,1024]{1,0:T(8,128)(4,1)S(1)} %get-tuple-element.151) | copy-start | bytes 1572868
  73.4 6.4 copy-start.31
  73.5 8.3 copy-start.26
  86.5 124.5 %copy-start.78 = (f32[768]{0:T(1024)S(1)}, f32[768]{0:T(1024)}, u32[]{:S(2)}) copy-start(f32[768]{0:T(1024)} %param.26) | copy-start | bytes 9220
  89.1 127.1 %all-gather.3.cloned.1.call-start = ((), (), s32[]{:S(2)}) async-start(), calls=%async_computation.6 | async-start | bytes 1327104 | tf_op jit(solution)/shard_map/all_gather | solution.py:24
  89.7 149.2 %all-gather.5.cloned.1.call-start = ((), (), s32[]{:S(2)}) async-start(), calls=%async_computation.7 | async-start | bytes 1327104 | tf_op jit(solution)/shard_map/all_gather | solution.py:25
  90.3 276.3 %all-reduce.14.cloned.1.call-start = ((), (), s32[]{:S(2)}) async-start(), calls=%async_computation.16 | async-start | bytes 6291456 | tf_op jit(solution)/shard_map/psum | solution.py:172
  245.9 269.9 %all-reduce.12.cloned.1.call-start = ((), (), s32[]{:S(2)}) async-start(), calls=%async_computation.15 | async-start | bytes 6291456 | tf_op jit(solution)/shard_map/psum | solution.py:193
  395.2 287.9 %reduce-scatter.25.cloned.1.call-start = ((), (), s32[]{:S(2)}) async-start(), calls=%async_computation.13 | async-start | bytes 884736
  515.8 9.5 %copy-start.10 = (bf16[1024,768]{1,0:T(8,128)(2,1)S(1)}, bf16[1024,768]{1,0:T(8,128)(2,1)}, u32[]{:S(2)}) copy-start(bf16[1024,768]{1,0:T(8,128)(2,1)} %get-tuple-element.114) | copy-start | bytes 4718596
  515.8 9.5 %copy-start.14 = (bf16[1024,768]{1,0:T(8,128)(2,1)S(1)}, bf16[1024,768]{1,0:T(8,128)(2,1)}, u32[]{:S(2)}) copy-start(bf16[1024,768]{1,0:T(8,128)(2,1)} %get-tuple-element.115) | copy-start | bytes 4718596
  515.8 9.5 %copy-start.16 = (f32[1024,768]{1,0:T(8,128)S(1)}, f32[1024,768]{1,0:T(8,128)}, u32[]{:S(2)}) copy-start(f32[1024,768]{1,0:T(8,128)} %copy-done.15) | copy-start | bytes 9437188
  515.8 9.5 %copy-start.19 = (f32[1024,768]{1,0:T(8,128)S(1)}, f32[1024,768]{1,0:T(8,128)}, u32[]{:S(2)}) copy-start(f32[1024,768]{1,0:T(8,128)} %copy-done.18) | copy-start | bytes 9437188
  515.8 9.5 %copy-start.39 = (bf16[1024,768]{1,0:T(8,128)(2,1)S(1)}, bf16[1024,768]{1,0:T(8,128)(2,1)}, u32[]{:S(2)}) copy-start(bf16[1024,768]{1,0:T(8,128)(2,1)} %get-tuple-element.110) | copy-start | bytes 4718596
  515.8 9.5 %copy-start.90 = (f32[1024]{0:T(1024)S(1)}, f32[1024]{0:T(1024)}, u32[]{:S(2)}) copy-start(f32[1024]{0:T(1024)} %add_rsqrt_fusion.1) | copy-start | bytes 12292
  515.9 9.5 %copy-start.96 = (f32[768]{0:T(1024)S(1)}, f32[768]{0:T(1024)}, u32[]{:S(2)}) copy-start(f32[768]{0:T(1024)} %param.27) | copy-start | bytes 9220
  515.9 18.7 %slice-start.4 = ((s8[6291456]{0:T(1024)(128)(4,1)}), s8[4194304]{0:T(1024)(128)(4,1)S(1)}, s32[]{:S(2)}) async-start(s8[6291456]{0:T(1024)(128)(4,1)} %bitcast.113), calls=%async_computation.22 | async-start | bytes 8388608
  525.4 9.2 %slice-start.5 = ((s8[6291456]{0:T(1024)(128)(4,1)}), s8[2097152]{0:T(1024)(128)(4,1)S(1)}, s32[]{:S(2)}) async-start(s8[6291456]{0:T(1024)(128)(4,1)} %bitcast.113), calls=%async_computation.23 | async-start | bytes 4194304
  534.5 7.3 copy-start.74
  546.1 8.4 %copy-start.37 = (bf16[192,1024]{1,0:T(8,128)(2,1)S(1)}, bf16[192,1024]{1,0:T(8,128)(2,1)}, u32[]{:S(2)}) copy-start(bf16[192,1024]{1,0:T(8,128)(2,1)} %convolution_convert_fusion.8) | copy-start | bytes 1179652
  546.1 12.3 %copy-start.63 = (bf16[192,1024]{1,0:T(8,128)(2,1)S(1)}, bf16[192,1024]{1,0:T(8,128)(2,1)}, u32[]{:S(2)}) copy-start(bf16[192,1024]{1,0:T(8,128)(2,1)} %fusion.50) | copy-start | bytes 1179652
  546.1 13.9 %copy-start.88 = (f32[3,512]{1,0:T(4,128)S(1)}, f32[3,512]{1,0:T(4,128)}, u32[]{:S(2)}) copy-start(f32[3,512]{1,0:T(4,128)} %copy-done.87) | copy-start | bytes 18436
  554.6 11.2 %slice-start.2 = ((s8[6291456]{0:T(1024)(128)(4,1)}), s8[4194304]{0:T(1024)(128)(4,1)S(1)}, s32[]{:S(2)}) async-start(s8[6291456]{0:T(1024)(128)(4,1)} %bitcast.111), calls=%async_computation.20 | async-start | bytes 8388608
  560.1 10.2 %slice-start.6 = ((s8[6291456]{0:T(1024)(128)(4,1)}), s8[4194304]{0:T(1024)(128)(4,1)S(1)}, s32[]{:S(2)}) async-start(s8[6291456]{0:T(1024)(128)(4,1)} %bitcast.115), calls=%async_computation.24 | async-start | bytes 8388608
  574.7 8.2 copy-start.35
  591.9 145.2 %all-reduce.10.cloned.1.call-start = ((), (), s32[]{:S(2)}) async-start(), calls=%async_computation.14 | async-start | bytes 6291456 | tf_op jit(solution)/shard_map/psum | solution.py:250
  598.2 14.5 %copy-start.57 = (bf16[3,64,1024]{2,1,0:T(8,128)(2,1)}, bf16[3,64,1024]{2,1,0:T(8,128)(2,1)S(1)}, u32[]{:S(2)}) copy-start(bf16[3,64,1024]{2,1,0:T(8,128)(2,1)S(1)} %get-tuple-element.176) | copy-start | bytes 1179652
  603.8 10.8 %copy-start.77 = (bf16[3,64,1024]{2,1,0:T(8,128)(2,1)}, bf16[3,64,1024]{2,1,0:T(8,128)(2,1)S(1)}, u32[]{:S(2)}) copy-start(bf16[3,64,1024]{2,1,0:T(8,128)(2,1)S(1)} %get-tuple-element.174) | copy-start | bytes 1179652
  616.5 126.7 %reduce-scatter.17.cloned.1.call-start = ((), (), s32[]{:S(2)}) async-start(), calls=%async_computation.9 | async-start | bytes 2654208 | tf_op jit(solution)/shard_map/reduce_scatter | solution.py:36
  623.8 119.4 %reduce-scatter.15.cloned.1.call-start = ((), (), s32[]{:S(2)}) async-start(), calls=%async_computation.8 | async-start | bytes 2654208 | tf_op jit(solution)/shard_map/reduce_scatter | solution.py:35
  631.4 126.5 %reduce-scatter.23.cloned.1.call-start = ((), (), s32[]{:S(2)}) async-start(), calls=%async_computation.12 | async-start | bytes 884736
  634.3 6.4 copy-start.49
  636.6 159.8 %reduce-scatter.19.cloned.1.call-start = ((), (), s32[]{:S(2)}) async-start(), calls=%async_computation.10 | async-start | bytes 884736
  644.3 190.7 %reduce-scatter.21.cloned.1.call-start = ((), (), s32[]{:S(2)}) async-start(), calls=%async_computation.11 | async-start | bytes 884736
  644.4 6.6 copy-start.45
  649.5 6.4 copy-start.104
  649.5 6.4 copy-start.105
  (106 other events, 377.3 us)
Sparse Core Ops, SparseCore 0:
  89.2 121.7 all-reduce.15
  246.0 120.4 all-reduce.13
  395.3 120.4 all-reduce.11
  616.6 120.4 all-reduce.9
Sparse Core Ops, SparseCore 1:
  91.4 24.1 all-gather.2
  117.4 23.9 all-gather.4
  592.0 34.0 reduce-scatter.24
  630.0 42.3 reduce-scatter.16
  676.7 42.4 reduce-scatter.14
  722.9 34.9 reduce-scatter.22
  761.4 34.9 reduce-scatter.18
  800.0 34.9 reduce-scatter.20
where the time goes:
time: 849 us; the launch traced here: 842 us
  waiting for transfers between devices  507 us (60%)
  matrix products  153 us (18%)
  other arithmetic  75.2 us (9%)
  blocking collectives  65.8 us (8%)
  local copies, waits for them, and re-layouts  22.8 us (3%)
  between operations  17.1 us (2%)
    psum x1, waiting for transfers between devices, body(): lax.psum(contract_rows(mixed_cols, full_o).astype(jnp.bfloat16), 'tensor')  121 us
    psum x1, waiting for transfers between devices, body(): lax.psum(jnp.dot(hidden, full_second, preferred_element_type=jnp.float32)...  121 us
    psum x1, waiting for transfers between devices, body(): lax.psum(contract_cols(grad_inner, full_first).astype(jnp.bfloat16), 'ten...  121 us
    unnamed x16, waiting for transfers between devices  93 us
    psum x1, waiting for transfers between devices, body(): lax.psum(back_terms.astype(jnp.bfloat16), 'tensor').astype(jnp.float32)  52.3 us
    psum x1, blocking collectives, reduce_small(): lax.psum((grads[0], grads[1], grads[2], grads[3], grads[4], grads[5], gra...  26.5 us
    dot_general x12, matrix products, contract_cols(): lax.dot_general(left, right, (((1,), (1,)), ((), ())), preferred_element_...  21.3 us
    dot_general x2, matrix products, body(): jnp.dot(first_low, full_first, preferred_element_type=jnp.float32) + b1  21 us
  transfers between devices with their start and end apart: 12, of which 7 were waited for; matrix products, arithmetic and copies ran while one was open for 11% of the time, Pallas kernels for 0%

commit v1 on v0

--- a/solution.py
+++ b/solution.py
@@ -162,8 +162,8 @@
             )
             log_totals.append(log_total)
         mixed_cols = jnp.concatenate(pieces, axis=2).reshape(width, seq_len).astype(jnp.bfloat16)
-        attended = lax.psum(
-            contract_rows(mixed_cols, full_o).astype(jnp.bfloat16), "tensor"
+        attended = jnp.sum(
+            lax.all_gather(contract_rows(mixed_cols, full_o).astype(jnp.bfloat16), "tensor"), axis=0
         ).astype(jnp.float32)
         first, normed_one, scaled_one = norm_forward(inputs + attended + bo, gain1, shift1)
         first_low = first.astype(jnp.bfloat16)

time: 849 us -> 1080 us (1.27)
  waiting for transfers between devices: 507 us -> 731 us
    all_gather x0 -> x2, waiting for transfers between devices: none -> 206 us  [body(): lax.all_gather(contract_rows(mixed_cols, full_o).astype(jnp.bfloat16), 't...]
    psum x1 -> x0, waiting for transfers between devices: 121 us -> none  [body(): lax.psum(contract_rows(mixed_cols, full_o).astype(jnp.bfloat16), 'tensor')]
    reduce_scatter x1, waiting for transfers between devices: 0.01 us -> 46.7 us  [reduce_large(): lax.psum_scatter(grads[4], 'dp', scatter_dimension=0, tiled=True)]
    reduce_scatter x1, waiting for transfers between devices: 0.01 us -> 39.4 us  [reduce_large(): lax.psum_scatter(grads[5], 'dp', scatter_dimension=1, tiled=True)]
    unnamed x16 -> x17, waiting for transfers between devices: 93 us -> 117 us
    all_gather x1, waiting for transfers between devices: 0.01 us -> 13.6 us  [collect(): lax.all_gather(w1, 'dp', axis=0, tiled=True)]
    unnamed x290 -> x274, local copies, waits for them, and re-layouts: 20.9 us -> 21.8 us
  transfers between devices with their start and end apart: 12 -> 13, of which waited for: 7 -> 12; matrix products, arithmetic and copies ran while one was open for 11% -> 12% of each run, Pallas kernels for 0% -> 0%
where the time goes in v1:
time: 1080 us; the launch traced here: 1070 us
  waiting for transfers between devices  731 us (68%)
  matrix products  151 us (14%)
  other arithmetic  84.3 us (8%)
  blocking collectives  66.1 us (6%)
  local copies, waits for them, and re-layouts  23.9 us (2%)
  between operations  15.7 us (1%)
    all_gather x2, waiting for transfers between devices, body(): lax.all_gather(contract_rows(mixed_cols, full_o).astype(jnp.bfloat16), 't...  206 us
    psum x1, waiting for transfers between devices, body(): lax.psum(jnp.dot(hidden, full_second, preferred_element_type=jnp.float32)...  121 us
    psum x1, waiting for transfers between devices, body(): lax.psum(contract_cols(grad_inner, full_first).astype(jnp.bfloat16), 'ten...  120 us
    unnamed x17, waiting for transfers between devices  117 us
    psum x1, waiting for transfers between devices, body(): lax.psum(back_terms.astype(jnp.bfloat16), 'tensor').astype(jnp.float32)  63 us
    reduce_scatter x1, waiting for transfers between devices, reduce_large(): lax.psum_scatter(grads[4], 'dp', scatter_dimension=0, tiled=True)  46.7 us
    reduce_scatter x1, waiting for transfers between devices, reduce_large(): lax.psum_scatter(grads[5], 'dp', scatter_dimension=1, tiled=True)  39.4 us
    psum x1, blocking collectives, reduce_small(): lax.psum((grads[0], grads[1], grads[2], grads[3], grads[4], grads[5], gra...  26.8 us
  transfers between devices with their start and end apart: 13, of which 12 were waited for; matrix products, arithmetic and copies ran while one was open for 12% of the time, Pallas kernels for 0%

profile of v1, /device:TPU:0, one launch (start us, length us, event | category | flops | bytes accessed | tf_op | source)
XLA Modules:
  0.0 1074.6 jit_solution(2197786599725825847)
XLA Ops:
  9.9 11.4 %all_gather.23 = bf16[192,768]{0,1:T(8,128)(2,1)S(1)} all-gather(bf16[192,96]{0,1:T(8,128)(2,1)} %copy.42), channel_id=1, replica_groups=mesh['dp'=8,'tensor'=4] {'dp'}, dimensions={1}, use_global_device_ids=true | all-gather | bytes 331776 | tf_op jit(solution)/shard_map/all_gather | solution.py:23
  21.3 9.3 all_gather.21
  30.6 8.8 all_gather.22
  39.5 9.8 all_gather.20
  86.4 95.9 %all-gather.13.cloned.1.call-done = bf16[4096,768]{1,0:T(8,128)(2,1)} async-done(((bf16[1024,768]{1,0:T(8,128)(2,1)}), bf16[4096,768]{1,0:T(8,128)(2,1)}) %all-gather.13.cloned.1.call-update) | async-done | bytes 6291472 | tf_op jit(solution)/shard_map/all_gather | solution.py:166
  182.3 5.3 reduce_sum.439
  187.6 110.5 %all-gather.11.cloned.1.call-done = bf16[4096,768]{1,0:T(8,128)(2,1)} async-done(((bf16[1024,768]{1,0:T(8,128)(2,1)}), bf16[4096,768]{1,0:T(8,128)(2,1)}) %all-gather.11.cloned.1.call-update) | async-done | bytes 6291472 | tf_op jit(solution)/shard_map/all_gather | solution.py:166
  298.1 5.3 reduce_sum.431
  308.7 13.6 %all-gather.7.cloned.1.call-done = bf16[768,768]{1,0:T(8,128)(2,1)} async-done(((bf16[96,768]{1,0:T(8,128)(2,1)}), bf16[768,768]{1,0:T(8,128)(2,1)}) %all-gather.7.cloned.1.call-update) | async-done | bytes 1179664 | tf_op jit(solution)/shard_map/all_gather | solution.py:24
  322.3 3.8 fusion.68
  327.9 17.1 %multiply_convert_fusion.5 = (bf16[1024,768]{1,0:T(8,128)(2,1)}, f32[1024,768]{1,0:T(8,128)}, bf16[1024,768]{1,0:T(8,128)(2,1)}, f32[1024,768]{1,0:T(8,128)}, f32[1024,768]{1,0:T(8,128)}) fusion(f32[768]{0:T(1024)S(1)} %copy-done.110, f32[1024,768]{1,0:T(8,128)S(1)} %fusion.68, bf16[768,768]{1,0:T(8,128)(2,1)S(1)} %copy-done.106, f32[768]{0:T(1024)S(1)} %copy-done.102, ...), kind=kOutput, calls=%fused_computation.92 | convolution fusion | flops 1318846464 | bytes 20078592 | tf_op jit(solution)/shard_map/dot_general | solution.py:170
  345.0 3.1 all-gather.9.cloned.1.call-done
  348.1 4.4 convolution_convert_fusion.4
  352.6 2.6 convolution_convert_fusion.2
  355.7 121.1 %all-reduce.12.cloned.1.call-done = (bf16[1024,768]{1,0:T(8,128)(2,1)}, bf16[1024,768]{1,0:T(8,128)(2,1)}) async-done(((bf16[1024,768]{1,0:T(8,128)(2,1)}, bf16[1024,768]{1,0:T(8,128)(2,1)}), (bf16[1024,768]{1,0:T(8,128)(2,1)}, bf16[1024,768]{1,0:T(8,128)(2,1)})) %all-reduce.12.cloned.1.call-update) | async-done | bytes 3145744 | tf_op jit(solution)/shard_map/psum | solution.py:172
  476.8 5.0 fusion.131
  483.7 3.5 convert_reduce_fusion
  487.3 4.4 fusion.18
  491.7 2.9 convert_reduce_fusion.2
  498.5 2.9 convert_reduce_fusion.3
  505.4 120.4 %all-reduce.10.cloned.1.call-done = (bf16[1024,768]{1,0:T(8,128)(2,1)}, bf16[1024,768]{1,0:T(8,128)(2,1)}) async-done(((bf16[1024,768]{1,0:T(8,128)(2,1)}, bf16[1024,768]{1,0:T(8,128)(2,1)}), (bf16[1024,768]{1,0:T(8,128)(2,1)}, bf16[1024,768]{1,0:T(8,128)(2,1)})) %all-reduce.10.cloned.1.call-update) | async-done | bytes 3145744 | tf_op jit(solution)/shard_map/psum | solution.py:193
  625.8 9.2 multiply_reduce_fusion.5
  635.1 5.3 fusion.130
  644.3 2.8 fusion.77
  647.1 4.4 multiply_reduce_fusion
  651.5 4.3 multiply_reduce_fusion.1
  655.9 8.4 multiply_convert_fusion
  664.3 3.8 convolution_multiply_fusion.1
  669.8 5.7 fusion.84
  675.6 4.5 multiply_reduce_fusion.2
  680.0 4.4 multiply_reduce_fusion.3
  684.4 8.2 multiply_convert_fusion.2
  692.7 3.8 convolution_multiply_fusion.3
  702.2 5.8 convert_reduce_fusion.4
  708.0 5.6 convert_reduce_fusion.5
  726.5 4.0 fusion.61
  730.5 3.0 convolution_add_fusion
  733.6 4.0 fusion.70
  737.7 3.5 convolution_add_fusion.1
  756.2 3.8 pad_maximum_fusion
  768.4 26.8 %all-reduce = (f32[192]{0:T(256)}, f32[192]{0:T(256)}, f32[768]{0:T(1024)}, f32[768]{0:T(1024)}, f32[768]{0:T(1024)}, /*index=5*/f32[768]{0:T(1024)}, f32[768]{0:T(1024)}, f32[768]{0:T(1024)}, f32[768]{0:T(1024)}) all-reduce(f32[192]{0:T(256)} %reshape.373, f32[192]{0:T(256)} %reshape.374, ...), channel_id=1, replica_groups=mesh['dp'=8,'tensor'=4] {'dp'}, use_global_device_ids=true, to_apply=%region_43.44 | all-reduce | flops 5760 | bytes 46080 | tf_op jit(solution)/shard_map/psum | solution.py:41
  796.8 63.0 %all-reduce.8.cloned.1.call-done = (bf16[1024,768]{1,0:T(8,128)(2,1)}, bf16[1024,768]{1,0:T(8,128)(2,1)}) async-done(((bf16[1024,768]{1,0:T(8,128)(2,1)}, bf16[1024,768]{1,0:T(8,128)(2,1)}), (bf16[1024,768]{1,0:T(8,128)(2,1)}, bf16[1024,768]{1,0:T(8,128)(2,1)})) %all-reduce.8.cloned.1.call-update) | async-done | bytes 3145744 | tf_op jit(solution)/shard_map/psum | solution.py:250
  859.8 2.8 add_convert_fusion.3
  865.8 39.4 %reduce-scatter.17.cloned.1.call-done = f32[768,96]{0,1:T(8,128)} async-done(((f32[768,768]{0,1:T(8,128)}), f32[768,96]{0,1:T(8,128)}) %reduce-scatter.17.cloned.1.call-update) | async-done | bytes 294928 | tf_op jit(solution)/shard_map/reduce_scatter | solution.py:36
  905.2 46.7 %reduce-scatter.15.cloned.1.call-done = f32[96,768]{1,0:T(8,128)} async-done(((f32[768,768]{1,0:T(8,128)}), f32[96,768]{1,0:T(8,128)}) %reduce-scatter.15.cloned.1.call-update) | async-done | bytes 294928 | tf_op jit(solution)/shard_map/reduce_scatter | solution.py:35
  951.9 38.7 %reduce-scatter.23.cloned.1.call-done = f32[96,192]{1,0:T(8,128)} async-done(((f32[768,192]{1,0:T(8,128)}), f32[96,192]{1,0:T(8,128)}) %reduce-scatter.23.cloned.1.call-update) | async-done | bytes 73744
  990.6 38.6 %reduce-scatter.19.cloned.1.call-done = f32[96,192]{1,0:T(8,128)} async-done(((f32[768,192]{1,0:T(8,128)}), f32[96,192]{1,0:T(8,128)}) %reduce-scatter.19.cloned.1.call-update) | async-done | bytes 73744
  1029.2 38.7 %reduce-scatter.21.cloned.1.call-done = f32[96,192]{1,0:T(8,128)} async-done(((f32[768,192]{1,0:T(8,128)}), f32[96,192]{1,0:T(8,128)}) %reduce-scatter.21.cloned.1.call-update) | async-done | bytes 73744
  (400 shorter events, 108.6 us)
Async XLA Ops:
  7.2 44.3 %copy-start = (bf16[2048,768]{1,0:T(8,128)(2,1)S(1)}, bf16[2048,768]{1,0:T(8,128)(2,1)}, u32[]{:S(2)}) copy-start(bf16[2048,768]{1,0:T(8,128)(2,1)} %param.18) | copy-start | bytes 9437188
  7.2 175.1 %all-gather.13.cloned.1.call-start = ((), (), s32[]{:S(2)}) async-start(), calls=%async_computation.9 | async-start | bytes 7864320 | tf_op jit(solution)/shard_map/all_gather | solution.py:166
  9.9 41.6 %copy-start.112 = (f32[192]{0:T(256)S(1)}, f32[192]{0:T(256)}, u32[]{:S(2)}) copy-start(f32[192]{0:T(256)} %param.21) | copy-start | bytes 2308
  30.6 21.7 %copy-start.48 = (bf16[768,192]{1,0:T(8,128)(2,1)}, bf16[768,192]{1,0:T(8,128)(2,1)S(1)}, u32[]{:S(2)}) copy-start(bf16[768,192]{1,0:T(8,128)(2,1)S(1)} %all_gather.21) | copy-start | bytes 884740
  39.4 13.5 %copy-start.50 = (bf16[768,192]{1,0:T(8,128)(2,1)}, bf16[768,192]{1,0:T(8,128)(2,1)S(1)}, u32[]{:S(2)}) copy-start(bf16[768,192]{1,0:T(8,128)(2,1)S(1)} %all_gather.22) | copy-start | bytes 884740
  49.3 10.0 copy-start.40
  52.9 7.1 copy-start.29
  53.0 9.0 copy-start.24
  66.5 231.6 %all-gather.11.cloned.1.call-start = ((), (), s32[]{:S(2)}) async-start(), calls=%async_computation.8 | async-start | bytes 7864320 | tf_op jit(solution)/shard_map/all_gather | solution.py:166
  71.3 7.1 copy-start.31
  71.3 9.0 copy-start.26
  84.8 237.5 %all-gather.7.cloned.1.call-start = ((), (), s32[]{:S(2)}) async-start(), calls=%async_computation.6 | async-start | bytes 1327104 | tf_op jit(solution)/shard_map/all_gather | solution.py:24
  85.6 262.6 %all-gather.9.cloned.1.call-start = ((), (), s32[]{:S(2)}) async-start(), calls=%async_computation.7 | async-start | bytes 1327104 | tf_op jit(solution)/shard_map/all_gather | solution.py:25
  86.2 390.7 %all-reduce.12.cloned.1.call-start = ((), (), s32[]{:S(2)}) async-start(), calls=%async_computation.18 | async-start | bytes 6291456 | tf_op jit(solution)/shard_map/psum | solution.py:172
  355.2 270.5 %all-reduce.10.cloned.1.call-start = ((), (), s32[]{:S(2)}) async-start(), calls=%async_computation.17 | async-start | bytes 6291456 | tf_op jit(solution)/shard_map/psum | solution.py:193
  505.1 290.0 %reduce-scatter.25.cloned.1.call-start = ((), (), s32[]{:S(2)}) async-start(), calls=%async_computation.15 | async-start | bytes 884736
  625.7 9.2 copy-start.6
  625.7 9.2 copy-start.10
  625.8 9.3 copy-start.16
  625.8 9.3 copy-start.19
  625.8 9.3 copy-start.39
  625.8 9.3 copy-start.85
  625.8 9.3 copy-start.88
  625.8 18.4 %slice-start.2 = ((s8[6291456]{0:T(1024)(128)(4,1)}), s8[4194304]{0:T(1024)(128)(4,1)S(1)}, s32[]{:S(2)}) async-start(s8[6291456]{0:T(1024)(128)(4,1)} %bitcast.113), calls=%async_computation.21 | async-start | bytes 8388608
  635.1 9.2 slice-start.3
  644.2 7.3 copy-start.71
  655.9 8.4 copy-start.35
  655.9 12.2 %copy-start.57 = (bf16[192,1024]{1,0:T(8,128)(2,1)S(1)}, bf16[192,1024]{1,0:T(8,128)(2,1)}, u32[]{:S(2)}) copy-start(bf16[192,1024]{1,0:T(8,128)(2,1)} %copy-done.56) | copy-start | bytes 1179652
  655.9 13.9 %copy-start.84 = (f32[3,512]{1,0:T(4,128)S(1)}, f32[3,512]{1,0:T(4,128)}, u32[]{:S(2)}) copy-start(f32[3,512]{1,0:T(4,128)} %copy-done.83) | copy-start | bytes 18436
  664.3 11.2 %slice-start.4 = ((s8[6291456]{0:T(1024)(128)(4,1)}), s8[4194304]{0:T(1024)(128)(4,1)S(1)}, s32[]{:S(2)}) async-start(s8[6291456]{0:T(1024)(128)(4,1)} %bitcast.115), calls=%async_computation.23 | async-start | bytes 8388608
  669.7 5.8 copy-start.27
  669.7 5.8 copy-start.68
  669.8 10.3 slice-start.6
  684.4 8.2 copy-start.37
  701.7 158.1 %all-reduce.8.cloned.1.call-start = ((), (), s32[]{:S(2)}) async-start(), calls=%async_computation.16 | async-start | bytes 6291456 | tf_op jit(solution)/shard_map/psum | solution.py:250
  702.1 5.8 copy-start.28
  702.1 5.8 copy-start.70
  702.1 5.8 copy-start.82
  702.2 5.8 copy-start.117
  708.0 14.6 %copy-start.55 = (bf16[3,64,1024]{2,1,0:T(8,128)(2,1)}, bf16[3,64,1024]{2,1,0:T(8,128)(2,1)S(1)}, u32[]{:S(2)}) copy-start(bf16[3,64,1024]{2,1,0:T(8,128)(2,1)S(1)} %get-tuple-element.174) | copy-start | bytes 1179652
  713.6 10.8 %copy-start.74 = (bf16[3,64,1024]{2,1,0:T(8,128)(2,1)}, bf16[3,64,1024]{2,1,0:T(8,128)(2,1)S(1)}, u32[]{:S(2)}) copy-start(bf16[3,64,1024]{2,1,0:T(8,128)(2,1)S(1)} %get-tuple-element.172) | copy-start | bytes 1179652
  726.2 179.0 %reduce-scatter.17.cloned.1.call-start = ((), (), s32[]{:S(2)}) async-start(), calls=%async_computation.11 | async-start | bytes 2654208 | tf_op jit(solution)/shard_map/reduce_scatter | solution.py:36
  733.5 218.4 %reduce-scatter.15.cloned.1.call-start = ((), (), s32[]{:S(2)}) async-start(), calls=%async_computation.10 | async-start | bytes 2654208 | tf_op jit(solution)/shard_map/reduce_scatter | solution.py:35
  741.2 249.4 %reduce-scatter.23.cloned.1.call-start = ((), (), s32[]{:S(2)}) async-start(), calls=%async_computation.14 | async-start | bytes 884736
  747.5 281.7 %reduce-scatter.19.cloned.1.call-start = ((), (), s32[]{:S(2)}) async-start(), calls=%async_computation.12 | async-start | bytes 884736
  756.1 311.8 %reduce-scatter.21.cloned.1.call-start = ((), (), s32[]{:S(2)}) async-start(), calls=%async_computation.13 | async-start | bytes 884736
  761.3 6.4 copy-start.96
  761.3 6.4 copy-start.97
  (99 other events, 359.2 us)
Sparse Core Ops, SparseCore 0:
  66.6 115.6 all-gather.12
  184.5 113.5 all-gather.10
  300.0 22.2 all-gather.6
  324.0 24.0 all-gather.8
  355.3 121.4 all-reduce.11
  505.3 120.4 all-reduce.9
  701.8 34.0 reduce-scatter.24
  738.3 121.4 all-reduce.7
  863.7 41.5 reduce-scatter.16
  909.4 42.4 reduce-scatter.14
  955.6 34.9 reduce-scatter.22
  994.2 34.9 reduce-scatter.18
  1032.9 34.9 reduce-scatter.20
